TPU v7x, 128 devices: a whole 4x4x4 slice. The times are simulated.
128 devices in a mesh: member: 2 (over y_hi), gridy: 8 (over x, core), gridx: 8 (over z, y_lo).
Axes of the slice: x: 4, y: 4 (y_hi: 2, y_lo: 2; y = y_hi * 2 + y_lo), z: 4, core: 2. Of those that a mesh axis runs over, the one named last changes fastest.
Arguments:
- temp: float32 [4, 4, 512, 2048], P('member', None, 'gridy', 'gridx'), may hold values from -6 to 6
- salt: float32 [4, 4, 512, 2048], P('member', None, 'gridy', 'gridx'), may hold values from -6 to 6
- uvel: float32 [4, 4, 512, 2048], P('member', None, 'gridy', 'gridx'), may hold values from -3 to 3
- vvel: float32 [4, 4, 512, 2048], P('member', None, 'gridy', 'gridx'), may hold values from -3 to 3
- eta: float32 [4, 512, 2048], P('member', 'gridy', 'gridx'), may hold values from -6 to 6
- land_mask: int32 [512, 2048], P('gridy', 'gridx'), may hold values 0 or 1
- clone_source: int32 [4], P('member'), may hold values from 0 to 3
Outputs:
- new_temp: float32 [4, 4, 512, 2048], P('member', None, 'gridy', 'gridx')
- new_salt: float32 [4, 4, 512, 2048], P('member', None, 'gridy', 'gridx')
- new_uvel: float32 [4, 4, 512, 2048], P('member', None, 'gridy', 'gridx')
- new_vvel: float32 [4, 4, 512, 2048], P('member', None, 'gridy', 'gridx')
- new_eta: float32 [4, 512, 2048], P('member', 'gridy', 'gridx')
- overturning: float32 [4, 4, 512], P('member', None, 'gridy')
- clone_weight: float32 [4], P('member')
All inputs are finite; a program needn't handle non-finite values. No bound on the sum of `land_mask` on one device may be relied on, other than what follows from the above.
Results may differ from a plain program's by a relative error of at most 0.0001.
Values sent between devices are 32-bit elements; how exact they have to be, the bound alone decides.
A program may use at most 128 MiB of HBM per device.

v0:
```python
import jax
import jax.numpy as jnp
from jax import lax
from jax.sharding import PartitionSpec as P

STEPS = 2
ITERS = 3
ALPHA_T = 0.8
BETA_S = 0.6
PRESS_K = 0.25
STEP_DT = 0.1
KAPPA = 0.1
VISCOSITY = 0.1
DRAG_K = 0.05
CORI_K = 1.0
SURF_C = 4.0
DIV_K = 0.5
GRAV_K = 0.5


def padded_2(block, sides, width):
    for axis, dim in sides:
        count = lax.axis_size(axis)
        forward = [(i, i + 1) for i in range(count - 1)]
        forward.append((count - 1, 0))
        backward = [(target, source) for source, target in forward]
        low = lax.ppermute(
            lax.slice_in_dim(block, block.shape[dim] - width, None, axis=dim), axis, forward
        )
        high = lax.ppermute(lax.slice_in_dim(block, 0, width, axis=dim), axis, backward)
        block = jnp.concatenate([low, block, high], axis=dim)
    return block


def pressure(temp, salt):
    return PRESS_K * jnp.cumsum(BETA_S * salt - ALPHA_T * temp, axis=-3)


def split_rims(padded, south_keep, north_keep):
    east_side = padded[..., 1:-1, 2:]
    west_side = padded[..., 1:-1, :-2]
    north_side = padded[..., 2:, 1:-1]
    south_side = padded[..., :-2, 1:-1]
    north_side = north_side.at[..., -1, :].multiply(north_keep)
    south_side = south_side.at[..., 0, :].multiply(south_keep)
    return (east_side, west_side, north_side, south_side)


def volume_sides(fields, south_keep, north_keep):
    padded = padded_2(jnp.stack(fields), (("gridy", 3), ("gridx", 4)), 1)
    return split_rims(padded, south_keep, north_keep)


def surface_sides(fields, south_keep, north_keep):
    padded = padded_2(jnp.stack(fields), (("gridy", 2), ("gridx", 3)), 1)
    return split_rims(padded, south_keep, north_keep)


def surface_apply(field, south_keep, north_keep):
    east_side, west_side, north_side, south_side = surface_sides((field,), south_keep, north_keep)
    return (1.0 + 4.0 * SURF_C) * field - SURF_C * (
        east_side[0] + west_side[0] + north_side[0] + south_side[0]
    )


def member_total(values):
    return jnp.sum(values, axis=(1, 2))


def squared_norm(residual):
    return lax.psum(member_total(residual * residual), ("gridy", "gridx"))


def widen(values):
    return values[:, None, None]


def surface_solve(rhs, south_keep, north_keep):
    solution = jnp.zeros_like(rhs)
    residual = rhs
    direction = rhs
    norm_now = squared_norm(residual)
    for count in range(ITERS):
        image = surface_apply(direction, south_keep, north_keep)
        alpha = norm_now / lax.psum(member_total(direction * image), ("gridy", "gridx"))
        solution = solution + widen(alpha) * direction
        residual = residual - widen(alpha) * image
        norm_next = squared_norm(residual)
        direction = residual + widen(norm_next / norm_now) * direction
        norm_now = norm_next
    return solution


def shards(temp, salt, uvel, vvel, eta, land_mask, clone_source):
    levels = temp.shape[1]
    rows = temp.shape[2]
    cols = temp.shape[3]
    ocean = land_mask.astype(jnp.float32)
    tile_row = lax.axis_index("gridy")
    tile_count = lax.axis_size("gridy")
    total_rows = rows * tile_count
    total_cols = cols * lax.axis_size("gridx")
    south_keep = (tile_row > 0).astype(jnp.float32)
    north_keep = (tile_row < tile_count - 1).astype(jnp.float32)
    latitude = (tile_row * rows + jnp.arange(rows, dtype=jnp.int32)).astype(jnp.float32) + 0.5
    coriolis = (CORI_K * (2.0 * latitude / total_rows - 1.0))[:, None]
    for count in range(STEPS):
        press = pressure(temp, salt)
        east_side, west_side, north_side, south_side = volume_sides(
            (temp, salt, uvel, vvel, press), south_keep, north_keep
        )
        lap_temp = east_side[0] + west_side[0] + north_side[0] + south_side[0] - 4.0 * temp
        lap_salt = east_side[1] + west_side[1] + north_side[1] + south_side[1] - 4.0 * salt
        lap_uvel = east_side[2] + west_side[2] + north_side[2] + south_side[2] - 4.0 * uvel
        lap_vvel = east_side[3] + west_side[3] + north_side[3] + south_side[3] - 4.0 * vvel
        temp_next = ocean * (
            temp
            - STEP_DT
            * 0.5
            * (uvel * (east_side[0] - west_side[0]) + vvel * (north_side[0] - south_side[0]))
            + KAPPA * lap_temp
        )
        salt_next = ocean * (
            salt
            - STEP_DT
            * 0.5
            * (uvel * (east_side[1] - west_side[1]) + vvel * (north_side[1] - south_side[1]))
            + KAPPA * lap_salt
        )
        ustar = ocean * (
            uvel
            + STEP_DT * (coriolis * vvel - 0.5 * (east_side[4] - west_side[4]) - DRAG_K * uvel)
            + VISCOSITY * lap_uvel
        )
        vstar = ocean * (
            vvel
            + STEP_DT * (-coriolis * uvel - 0.5 * (north_side[4] - south_side[4]) - DRAG_K * vvel)
            + VISCOSITY * lap_vvel
        )
        trans_u = jnp.sum(ustar, axis=1)
        trans_v = jnp.sum(vstar, axis=1)
        east_t, west_t, north_t, south_t = surface_sides((trans_u, trans_v), south_keep, north_keep)
        rhs = eta - DIV_K * 0.5 * (east_t[0] - west_t[0] + (north_t[1] - south_t[1]))
        eta = surface_solve(rhs, south_keep, north_keep)
        east_e, west_e, north_e, south_e = surface_sides((eta,), south_keep, north_keep)
        uvel = ocean * (ustar - GRAV_K * 0.5 * (east_e[0] - west_e[0])[:, None])
        vvel = ocean * (vstar - GRAV_K * 0.5 * (north_e[0] - south_e[0])[:, None])
        temp = temp_next
        salt = salt_next
    zonal_scale = 1.0 / jnp.sqrt(jnp.float32(total_cols))
    score_scale = 1.0 / jnp.sqrt(jnp.float32(levels * total_rows))
    lat_weight = latitude / total_rows
    zonal_local = jnp.sum(vvel, axis=3)
    zonal_whole = lax.psum(zonal_local, "gridx")
    overturn = jnp.cumsum(zonal_whole, axis=1) * zonal_scale
    score = lax.psum(jnp.sum(overturn * lat_weight, axis=(1, 2)) * score_scale, "gridy")
    state_stack = jnp.stack((temp, salt, uvel, vvel))
    every_state, every_eta, every_score = (
        lax.all_gather(state_stack, "member", axis=1, tiled=True),
        lax.all_gather(eta, "member", axis=0, tiled=True),
        lax.all_gather(score, "member", axis=0, tiled=True),
    )
    picked = jnp.take(every_state, clone_source, axis=1)
    new_eta = jnp.take(every_eta, clone_source, axis=0)
    clone_weight = jnp.take(every_score, clone_source, axis=0) - jnp.mean(every_score)
    return (picked[0], picked[1], picked[2], picked[3], new_eta, overturn, clone_weight)


def solution(mesh):
    in_specs = (
        P("member", None, "gridy", "gridx"),
        P("member", None, "gridy", "gridx"),
        P("member", None, "gridy", "gridx"),
        P("member", None, "gridy", "gridx"),
        P("member", "gridy", "gridx"),
        P("gridy", "gridx"),
        P("member"),
    )
    out_specs = (
        P("member", None, "gridy", "gridx"),
        P("member", None, "gridy", "gridx"),
        P("member", None, "gridy", "gridx"),
        P("member", None, "gridy", "gridx"),
        P("member", "gridy", "gridx"),
        P("member", None, "gridy"),
        P("member"),
    )
    return jax.shard_map(shards, mesh=mesh, in_specs=in_specs, out_specs=out_specs, check_vma=False)
```

profile of v0, /device:TPU:1, one launch (start us, length us, event | category | flops | bytes accessed | tf_op | source)
XLA Modules:
  0.0 1724.0 jit_solution(7264022242541431259)
XLA Ops:
  23.1 3.5 collective-permute-start.2
  26.7 3.0 pad_maximum_fusion.5
  37.6 2.9 fusion.179
  40.7 2.9 fusion.181
  43.6 4.2 collective-permute-start.5
  49.2 3.6 collective-permute-start.6
  57.2 3.4 collective-permute-start.9
  62.0 3.9 collective-permute-start.10
  68.0 133.2 %all-reduce.2 = (f32[2]{0:T(128)S(1)}, f32[2]{0:T(128)S(1)}) all-reduce(f32[2]{0:T(128)S(1)} %get-tuple-element.298, f32[2]{0:T(128)S(1)} %get-tuple-element.297), channel_id=1, replica_groups=mesh['member'=2,'gridy'=8,'gridx'=8] {'gridy','gridx'}, use_global_device_ids=true, to_apply=%region_4.5 | all-reduce | flops 4 | bytes 32 | tf_op jit(solution)/shard_map/psum | solution.py:71
  201.4 139.0 %psum.100 = f32[2]{0:T(128)S(1)} all-reduce(f32[2]{0:T(128)S(1)} %get-tuple-element.316), channel_id=1, replica_groups=mesh['member'=2,'gridy'=8,'gridx'=8] {'gridy','gridx'}, use_global_device_ids=true, to_apply=%region_8.9 | all-reduce | flops 2 | bytes 16 | tf_op jit(solution)/shard_map/psum | solution.py:71
  340.5 11.4 collective-permute-start.13
  358.8 133.5 %psum.101 = f32[2]{0:T(128)S(1)} all-reduce(f32[2]{0:T(128)S(1)} %get-tuple-element.314), channel_id=1, replica_groups=mesh['member'=2,'gridy'=8,'gridx'=8] {'gridy','gridx'}, use_global_device_ids=true, to_apply=%region_10.11 | all-reduce | flops 2 | bytes 16 | tf_op jit(solution)/shard_map/psum | solution.py:85
  492.5 139.0 %psum.102 = f32[2]{0:T(128)S(1)} all-reduce(f32[2]{0:T(128)S(1)} %multiply_reduce_fusion.5), channel_id=1, replica_groups=mesh['member'=2,'gridy'=8,'gridx'=8] {'gridy','gridx'}, use_global_device_ids=true, to_apply=%region_12.13 | all-reduce | flops 2 | bytes 16 | tf_op jit(solution)/shard_map/psum | solution.py:71
  632.1 11.4 collective-permute-start.17
  651.0 3.5 bitcast_dynamic-update-slice_fusion.3
  654.5 134.3 %psum.103 = f32[2]{0:T(128)} all-reduce(f32[2]{0:T(128)} %fusion.143), channel_id=1, replica_groups=mesh['member'=2,'gridy'=8,'gridx'=8] {'gridy','gridx'}, use_global_device_ids=true, to_apply=%region_14.15 | all-reduce | flops 2 | bytes 16 | tf_op jit(solution)/shard_map/psum | solution.py:85
  790.5 11.7 collective-permute-start.21
  802.2 3.5 bitcast_dynamic-update-slice_fusion.2
  805.9 3.6 collective-permute-start.22
  816.5 4.1 collective-permute-start.25
  824.4 2.5 copy.20
  826.9 2.5 copy.18
  829.4 3.9 collective-permute-start.26
  833.2 3.0 pad_maximum_fusion.3
  844.3 2.5 copy.19
  846.8 3.4 fusion.175
  850.3 3.0 fusion.173
  853.3 3.7 collective-permute-start.29
  859.0 3.6 collective-permute-start.30
  867.7 3.6 collective-permute-start.33
  873.2 3.6 collective-permute-start.34
  883.2 131.9 %all-reduce.1 = (f32[2]{0:T(128)}, f32[2]{0:T(128)}) all-reduce(f32[2]{0:T(128)} %get-tuple-element.296, f32[2]{0:T(128)} %get-tuple-element.295), channel_id=1, replica_groups=mesh['member'=2,'gridy'=8,'gridx'=8] {'gridy','gridx'}, use_global_device_ids=true, to_apply=%region_19.20 | all-reduce | flops 4 | bytes 32 | tf_op jit(solution)/shard_map/psum | solution.py:71
  1017.1 140.1 %psum.106 = f32[2]{0:T(128)S(1)} all-reduce(f32[2]{0:T(128)} %get-tuple-element.307), channel_id=1, replica_groups=mesh['member'=2,'gridy'=8,'gridx'=8] {'gridy','gridx'}, use_global_device_ids=true, to_apply=%region_23.24 | all-reduce | flops 2 | bytes 16 | tf_op jit(solution)/shard_map/psum | solution.py:71
  1158.9 11.7 collective-permute-start.37
  1172.7 3.4 collective-permute-start.38
  1183.0 131.7 %psum.107 = f32[2]{0:T(128)} all-reduce(f32[2]{0:T(128)} %get-tuple-element.305), channel_id=1, replica_groups=mesh['member'=2,'gridy'=8,'gridx'=8] {'gridy','gridx'}, use_global_device_ids=true, to_apply=%region_25.26 | all-reduce | flops 2 | bytes 16 | tf_op jit(solution)/shard_map/psum | solution.py:85
  1317.6 141.2 %psum.108 = f32[2]{0:T(128)} all-reduce(f32[2]{0:T(128)} %multiply_reduce_fusion), channel_id=1, replica_groups=mesh['member'=2,'gridy'=8,'gridx'=8] {'gridy','gridx'}, use_global_device_ids=true, to_apply=%region_27.28 | all-reduce | flops 2 | bytes 16 | tf_op jit(solution)/shard_map/psum | solution.py:71
  1460.6 11.8 collective-permute-start.41
  1474.3 3.6 collective-permute-start.42
  1484.5 131.7 %psum.109 = f32[2]{0:T(128)} all-reduce(f32[2]{0:T(128)} %fusion.107), channel_id=1, replica_groups=mesh['member'=2,'gridy'=8,'gridx'=8] {'gridy','gridx'}, use_global_device_ids=true, to_apply=%region_29.30 | all-reduce | flops 2 | bytes 16 | tf_op jit(solution)/shard_map/psum | solution.py:85
  1617.8 11.5 collective-permute-start.45
  1639.8 3.4 fusion.87
  1648.0 16.1 psum.110
  1664.8 9.2 all_gather.10
  1674.0 21.4 %psum.111 = f32[2]{0:T(128)S(1)} all-reduce(f32[2]{0:T(128)S(1)} %broadcast_multiply_fusion.9), channel_id=1, replica_groups=mesh['member'=2,'gridy'=8,'gridx'=8] {'gridy'}, use_global_device_ids=true, to_apply=%region_34.35 | all-reduce | flops 2 | bytes 16 | tf_op jit(solution)/shard_map/psum | solution.py:156
  1696.2 5.8 all-reduce
  1705.1 7.6 all-gather.2.cloned.1.call-done
  1712.7 2.9 gather_fusion
  (341 shorter events, 131.9 us)
Async XLA Ops:
  7.2 1705.5 %all-gather.2.cloned.1.call-start = ((), (), s32[]{:S(2)}) async-start(), calls=%async_computation | async-start | bytes 6291456 | tf_op jit(solution)/shard_map/all_gather | solution.py:159
  11.0 4.3 collective-permute-start.1
  12.5 3.0 collective-permute-start
  19.9 14.3 collective-permute-start.3
  23.1 12.8 collective-permute-start.2
  43.6 5.0 collective-permute-start.5
  47.8 1.2 collective-permute-start.4
  49.1 6.2 collective-permute-start.7
  49.2 6.9 collective-permute-start.6
  57.2 4.2 collective-permute-start.9
  60.6 1.2 collective-permute-start.8
  61.9 5.7 collective-permute-start.11
  62.0 5.7 collective-permute-start.10
  340.5 12.2 collective-permute-start.13
  351.9 1.2 collective-permute-start.12
  353.1 5.4 collective-permute-start.15
  354.9 3.6 collective-permute-start.14
  632.1 12.2 collective-permute-start.17
  643.5 1.2 collective-permute-start.16
  644.8 5.4 collective-permute-start.19
  646.7 3.5 collective-permute-start.18
  790.4 15.3 collective-permute-start.20
  790.5 15.2 collective-permute-start.21
  805.8 5.4 collective-permute-start.23
  805.9 5.3 collective-permute-start.22
  816.5 5.0 collective-permute-start.25
  820.6 1.2 collective-permute-start.24
  826.9 15.0 collective-permute-start.27
  829.4 14.9 collective-permute-start.26
  853.3 4.6 collective-permute-start.29
  857.0 1.2 collective-permute-start.28
  859.0 7.2 collective-permute-start.31
  859.0 7.3 collective-permute-start.30
  867.7 4.5 collective-permute-start.33
  871.3 1.2 collective-permute-start.32
  873.2 7.6 collective-permute-start.35
  873.2 8.2 collective-permute-start.34
  1158.9 12.5 collective-permute-start.37
  1170.6 1.2 collective-permute-start.36
  1172.5 8.1 collective-permute-start.39
  1172.7 8.0 collective-permute-start.38
  1460.6 12.6 collective-permute-start.41
  1472.4 1.2 collective-permute-start.40
  1474.3 8.2 collective-permute-start.43
  1474.3 8.2 collective-permute-start.42
  1617.8 12.3 collective-permute-start.45
  1630.6 5.4 collective-permute-start.47
  1632.4 3.6 collective-permute-start.46
  (54 other events, 674.5 us)
Sparse Core Ops, SparseCore 0:
  1646.8 65.7 all-gather.1
where the time goes:
time: 1730 us; the launch traced here: 1720 us
  blocking collectives  1410 us (82%)
  starting transfers between devices  137 us (8%)
  other arithmetic  72.2 us (4%)
  local copies, waits for them, and re-layouts  59.9 us (3%)
  waiting for transfers between devices  31 us (2%)
    psum x6, blocking collectives, squared_norm(): return lax.psum(member_total(residual * residual), ('gridy', 'gridx'))  825 us
    psum x4, blocking collectives, surface_solve(): lax.psum(member_total(direction * image), ('gridy', 'gridx'))  531 us
    ppermute x24, starting transfers between devices, padded_2(): lax.ppermute(lax.slice_in_dim(block, 0, width, axis=dim), axis, backward)  128 us
  transfers between devices with their start and end apart: 49, of which 31 were waited for; matrix products, arithmetic and copies ran while one was open for 3% of the time, Pallas kernels for 0%

commit v1 on v0

--- a/solution.py
+++ b/solution.py
@@ -82,7 +82,7 @@
     norm_now = squared_norm(residual)
     for count in range(ITERS):
         image = surface_apply(direction, south_keep, north_keep)
-        alpha = norm_now / lax.psum(member_total(direction * image), ("gridy", "gridx"))
+        alpha = norm_now / lax.psum(lax.psum(member_total(direction * image), "gridy"), "gridx")
         solution = solution + widen(alpha) * direction
         residual = residual - widen(alpha) * image
         norm_next = squared_norm(residual)

time: 1730 us -> 1350 us (0.78)
  blocking collectives: 1410 us -> 1050 us
    psum x4 -> x12, blocking collectives: 531 us -> 186 us  [the longest x6 96.6 us: surface_solve(): lax.psum(member_total(direction * image), 'gridy')]
  transfers between devices with their start and end apart: 49 -> 49, of which waited for: 31 -> 32; matrix products, arithmetic and copies ran while one was open for 3% -> 4% of each run, Pallas kernels for 0% -> 0%
where the time goes in v1:
time: 1350 us
  blocking collectives  1050 us (78%)
  starting transfers between devices  122 us (9%)
  other arithmetic  71.7 us (5%)
  local copies, waits for them, and re-layouts  59.9 us (4%)
  waiting for transfers between devices  31.6 us (2%)
  between operations  16.3 us (1%)
    psum x6, blocking collectives, squared_norm(): return lax.psum(member_total(residual * residual), ('gridy', 'gridx'))  810 us
    ppermute x24, starting transfers between devices, padded_2(): lax.ppermute(lax.slice_in_dim(block, 0, width, axis=dim), axis, backward)  111 us
    psum x6, blocking collectives, surface_solve(): lax.psum(member_total(direction * image), 'gridy')  96.6 us
    psum x6, blocking collectives, surface_solve(): lax.psum(lax.psum(member_total(direction * image), 'gridy'), 'gridx')  89.8 us
  transfers between devices with their start and end apart: 49, of which 32 were waited for; matrix products, arithmetic and copies ran while one was open for 4% of the time, Pallas kernels for 0%

profile of v1, /device:TPU:1, one launch (start us, length us, event | category | flops | bytes accessed | tf_op | source)
XLA Modules:
  0.0 1351.3 jit_solution(705025263639422169)
XLA Ops:
  23.1 3.5 collective-permute-start.2
  26.7 3.0 pad_maximum_fusion.5
  43.7 4.2 collective-permute-start.5
  49.3 3.6 collective-permute-start.6
  57.3 3.4 collective-permute-start.9
  62.1 3.9 collective-permute-start.10
  68.1 16.0 %psum.141 = f32[2]{0:T(128)S(1)} all-reduce(f32[2]{0:T(128)S(1)} %get-tuple-element.297), channel_id=1, replica_groups=mesh['member'=2,'gridy'=8,'gridx'=8] {'gridy'}, use_global_device_ids=true, to_apply=%region_6.7 | all-reduce | flops 2 | bytes 16 | tf_op jit(solution)/shard_map/psum | solution.py:85
  84.0 130.4 %psum.140 = f32[2]{0:T(128)S(1)} all-reduce(f32[2]{0:T(128)S(1)} %get-tuple-element.298), channel_id=1, replica_groups=mesh['member'=2,'gridy'=8,'gridx'=8] {'gridy','gridx'}, use_global_device_ids=true, to_apply=%region_4.5 | all-reduce | flops 2 | bytes 16 | tf_op jit(solution)/shard_map/psum | solution.py:71
  214.4 12.5 psum.142
  227.2 144.0 %psum.143 = f32[2]{0:T(128)S(1)} all-reduce(f32[2]{0:T(128)S(1)} %get-tuple-element.312), channel_id=1, replica_groups=mesh['member'=2,'gridy'=8,'gridx'=8] {'gridy','gridx'}, use_global_device_ids=true, to_apply=%region_9.10 | all-reduce | flops 2 | bytes 16 | tf_op jit(solution)/shard_map/psum | solution.py:71
  371.3 11.8 collective-permute-start.13
  384.4 3.6 collective-permute-start.14
  390.2 15.7 %psum.144 = f32[2]{0:T(128)S(1)} all-reduce(f32[2]{0:T(128)S(1)} %get-tuple-element.310), channel_id=1, replica_groups=mesh['member'=2,'gridy'=8,'gridx'=8] {'gridy'}, use_global_device_ids=true, to_apply=%region_11.12 | all-reduce | flops 2 | bytes 16 | tf_op jit(solution)/shard_map/psum | solution.py:85
  405.9 16.4 %psum.145 = f32[2]{0:T(128)S(1)} all-reduce(f32[2]{0:T(128)S(1)} %psum.144), channel_id=1, replica_groups=mesh['member'=2,'gridy'=8,'gridx'=8] {'gridx'}, use_global_device_ids=true, to_apply=%region_12.13 | all-reduce | flops 2 | bytes 16 | tf_op jit(solution)/shard_map/psum | solution.py:85
  422.5 131.1 %psum.146 = f32[2]{0:T(128)S(1)} all-reduce(f32[2]{0:T(128)S(1)} %multiply_reduce_fusion.5), channel_id=1, replica_groups=mesh['member'=2,'gridy'=8,'gridx'=8] {'gridy','gridx'}, use_global_device_ids=true, to_apply=%region_14.15 | all-reduce | flops 2 | bytes 16 | tf_op jit(solution)/shard_map/psum | solution.py:71
  554.3 11.7 collective-permute-start.17
  572.9 16.8 %psum.147 = f32[2]{0:T(128)} all-reduce(f32[2]{0:T(128)S(1)} %fusion.143), channel_id=1, replica_groups=mesh['member'=2,'gridy'=8,'gridx'=8] {'gridy'}, use_global_device_ids=true, to_apply=%region_16.17 | all-reduce | flops 2 | bytes 16 | tf_op jit(solution)/shard_map/psum | solution.py:85
  589.8 3.5 bitcast_dynamic-update-slice_fusion.3
  593.3 16.9 %psum.148 = f32[2]{0:T(128)} all-reduce(f32[2]{0:T(128)} %psum.147), channel_id=1, replica_groups=mesh['member'=2,'gridy'=8,'gridx'=8] {'gridx'}, use_global_device_ids=true, to_apply=%region_17.18 | all-reduce | flops 2 | bytes 16 | tf_op jit(solution)/shard_map/psum | solution.py:85
  616.3 3.5 bitcast_dynamic-update-slice_fusion.2
  620.0 3.6 collective-permute-start.22
  630.6 4.1 collective-permute-start.25
  643.5 3.9 collective-permute-start.26
  660.9 3.4 fusion.175
  664.3 3.0 fusion.173
  667.4 3.7 collective-permute-start.29
  673.1 3.6 collective-permute-start.30
  681.8 3.7 collective-permute-start.33
  687.3 3.6 collective-permute-start.34
  697.3 16.0 %psum.150 = f32[2]{0:T(128)} all-reduce(f32[2]{0:T(128)} %get-tuple-element.295), channel_id=1, replica_groups=mesh['member'=2,'gridy'=8,'gridx'=8] {'gridy'}, use_global_device_ids=true, to_apply=%region_24.25 | all-reduce | flops 2 | bytes 16 | tf_op jit(solution)/shard_map/psum | solution.py:85
  713.3 129.5 %psum.149 = f32[2]{0:T(128)} all-reduce(f32[2]{0:T(128)} %get-tuple-element.296), channel_id=1, replica_groups=mesh['member'=2,'gridy'=8,'gridx'=8] {'gridy','gridx'}, use_global_device_ids=true, to_apply=%region_22.23 | all-reduce | flops 2 | bytes 16 | tf_op jit(solution)/shard_map/psum | solution.py:71
  842.8 13.5 psum.151
  858.2 143.9 %psum.152 = f32[2]{0:T(128)S(1)} all-reduce(f32[2]{0:T(128)} %get-tuple-element.303), channel_id=1, replica_groups=mesh['member'=2,'gridy'=8,'gridx'=8] {'gridy','gridx'}, use_global_device_ids=true, to_apply=%region_27.28 | all-reduce | flops 2 | bytes 16 | tf_op jit(solution)/shard_map/psum | solution.py:71
  1003.8 11.4 collective-permute-start.37
  1027.6 16.0 %psum.153 = f32[2]{0:T(128)} all-reduce(f32[2]{0:T(128)} %get-tuple-element.301), channel_id=1, replica_groups=mesh['member'=2,'gridy'=8,'gridx'=8] {'gridy'}, use_global_device_ids=true, to_apply=%region_29.30 | all-reduce | flops 2 | bytes 16 | tf_op jit(solution)/shard_map/psum | solution.py:85
  1043.6 15.3 %psum.154 = f32[2]{0:T(128)} all-reduce(f32[2]{0:T(128)} %psum.153), channel_id=1, replica_groups=mesh['member'=2,'gridy'=8,'gridx'=8] {'gridx'}, use_global_device_ids=true, to_apply=%region_30.31 | all-reduce | flops 2 | bytes 16 | tf_op jit(solution)/shard_map/psum | solution.py:85
  1061.8 131.6 %psum.155 = f32[2]{0:T(128)} all-reduce(f32[2]{0:T(128)} %multiply_reduce_fusion), channel_id=1, replica_groups=mesh['member'=2,'gridy'=8,'gridx'=8] {'gridy','gridx'}, use_global_device_ids=true, to_apply=%region_32.33 | all-reduce | flops 2 | bytes 16 | tf_op jit(solution)/shard_map/psum | solution.py:71
  1195.1 11.7 collective-permute-start.41
  1218.9 16.0 %psum.156 = f32[2]{0:T(128)} all-reduce(f32[2]{0:T(128)} %fusion.107), channel_id=1, replica_groups=mesh['member'=2,'gridy'=8,'gridx'=8] {'gridy'}, use_global_device_ids=true, to_apply=%region_34.35 | all-reduce | flops 2 | bytes 16 | tf_op jit(solution)/shard_map/psum | solution.py:85
  1235.0 15.3 %psum.157 = f32[2]{0:T(128)} all-reduce(f32[2]{0:T(128)} %psum.156), channel_id=1, replica_groups=mesh['member'=2,'gridy'=8,'gridx'=8] {'gridx'}, use_global_device_ids=true, to_apply=%region_35.36 | all-reduce | flops 2 | bytes 16 | tf_op jit(solution)/shard_map/psum | solution.py:85
  1251.9 4.2 collective-permute-start.45
  1257.5 3.6 collective-permute-start.46
  1266.7 3.4 fusion.87
  1274.9 16.6 %psum.158 = f32[2,4,64]{2,1,0:T(4,128)S(1)} all-reduce(f32[2,4,64]{2,1,0:T(4,128)S(1)} %copy-done.41), channel_id=1, replica_groups=mesh['member'=2,'gridy'=8,'gridx'=8] {'gridx'}, use_global_device_ids=true, to_apply=%region_37.38 | all-reduce | flops 512 | bytes 4096 | tf_op jit(solution)/shard_map/psum | solution.py:154
  1292.2 9.2 all_gather.10
  1301.4 20.8 %psum.159 = f32[2]{0:T(128)S(1)} all-reduce(f32[2]{0:T(128)S(1)} %broadcast_multiply_fusion.9), channel_id=1, replica_groups=mesh['member'=2,'gridy'=8,'gridx'=8] {'gridy'}, use_global_device_ids=true, to_apply=%region_40.41 | all-reduce | flops 2 | bytes 16 | tf_op jit(solution)/shard_map/psum | solution.py:156
  1323.0 5.8 all-reduce
  1331.9 8.0 all-gather.2.cloned.1.call-done
  (349 shorter events, 155.1 us)
Async XLA Ops:
  7.2 1332.8 %all-gather.2.cloned.1.call-start = ((), (), s32[]{:S(2)}) async-start(), calls=%async_computation | async-start | bytes 6291456 | tf_op jit(solution)/shard_map/all_gather | solution.py:159
  11.0 4.3 collective-permute-start.1
  12.5 3.0 collective-permute-start
  19.9 14.3 %collective-permute-start.3 = (f32[5,2,4,66,1]{3,2,4,1,0:T(4,128)S(1)}, f32[5,2,4,66,1]{3,2,4,1,0:T(4,128)S(1)}, u32[]{:S(2)}, u32[]{:S(2)}) collective-permute-start(f32[5,2,4,66,1]{3,2,4,1,0:T(4,128)S(1)} %copy.16), channel_id=1, source_target_pairs={{0,1},{1,2},{2,3},{3,4},{4,5},{5,6},{6,7},{7,0},{8,9},{9,10},{10,1... | collective-permute-start | bytes 31688 | tf_op jit(solution)/shard_map/ppermute | solution.py:27
  23.1 12.9 collective-permute-start.2
  43.7 5.0 collective-permute-start.5
  47.9 1.2 collective-permute-start.4
  49.2 6.2 collective-permute-start.7
  49.3 6.9 collective-permute-start.6
  57.3 4.2 collective-permute-start.9
  60.7 1.2 collective-permute-start.8
  62.0 5.7 collective-permute-start.11
  62.1 5.7 collective-permute-start.10
  371.3 12.6 collective-permute-start.13
  383.0 1.2 collective-permute-start.12
  384.3 5.4 collective-permute-start.15
  384.4 5.6 collective-permute-start.14
  554.3 12.6 collective-permute-start.17
  566.0 1.2 collective-permute-start.16
  567.3 5.4 collective-permute-start.19
  569.4 3.3 collective-permute-start.18
  611.8 8.0 collective-permute-start.20
  614.4 5.4 collective-permute-start.21
  619.9 5.4 collective-permute-start.23
  620.0 5.3 collective-permute-start.22
  630.6 5.0 collective-permute-start.25
  634.7 1.2 collective-permute-start.24
  641.0 15.0 %collective-permute-start.27 = (f32[5,2,4,66,1]{3,2,4,1,0:T(4,128)}, f32[5,2,4,66,1]{3,2,4,1,0:T(4,128)}, u32[]{:S(2)}, u32[]{:S(2)}) collective-permute-start(f32[5,2,4,66,1]{3,2,4,1,0:T(4,128)} %copy.20), channel_id=1, source_target_pairs={{0,1},{1,2},{2,3},{3,4},{4,5},{5,6},{6,7},{7,0},{8,9},{9,10},{10,1... | collective-permute-start | bytes 31688 | tf_op jit(solution)/shard_map/ppermute | solution.py:27
  643.5 14.9 %collective-permute-start.26 = (f32[5,2,4,66,1]{3,2,4,1,0:T(4,128)}, f32[5,2,4,66,1]{3,2,4,1,0:T(4,128)}, u32[]{:S(2)}, u32[]{:S(2)}) collective-permute-start(f32[5,2,4,66,1]{3,2,4,1,0:T(4,128)} %copy.18), channel_id=1, source_target_pairs={{1,0},{2,1},{3,2},{4,3},{5,4},{6,5},{7,6},{0,7},{9,8},{10,9},{11,1... | collective-permute-start | bytes 31688 | tf_op jit(solution)/shard_map/ppermute | solution.py:30
  667.4 4.6 collective-permute-start.29
  671.1 1.2 collective-permute-start.28
  673.1 7.3 collective-permute-start.31
  673.1 7.3 collective-permute-start.30
  681.8 4.5 collective-permute-start.33
  685.4 1.2 collective-permute-start.32
  687.3 7.5 collective-permute-start.35
  687.3 8.1 collective-permute-start.34
  1003.8 12.2 collective-permute-start.37
  1015.2 1.2 collective-permute-start.36
  1017.1 8.2 collective-permute-start.39
  1018.3 6.9 collective-permute-start.38
  1195.1 12.6 collective-permute-start.41
  1206.9 1.2 collective-permute-start.40
  1208.8 8.2 collective-permute-start.43
  1210.8 6.2 collective-permute-start.42
  1251.9 5.0 collective-permute-start.45
  1257.4 5.4 collective-permute-start.47
  1257.5 5.3 collective-permute-start.46
  (54 other events, 658.6 us)
Sparse Core Ops, SparseCore 0:
  1273.7 66.1 all-gather.1
